TPU v7x, 256 devices: a whole 4x4x8 slice. The times are simulated.
256 devices in a mesh: grp: 8 (over x, z_lo), ref: 32 (over z_hi, y, core).
Axes of the slice: x: 4, y: 4, z: 8 (z_hi: 4, z_lo: 2; z = z_hi * 2 + z_lo), core: 2. Of those that a mesh axis runs over, the one named last changes fastest.
Arguments:
- particles: bfloat16 [2048, 512], P(('grp', 'ref')), may hold values from -30 to 30
- samples: bfloat16 [131072, 512], P('ref'), may hold values from -6 to 6
Outputs:
- moved: float32 [2048, 512], P(('grp', 'ref'))
All inputs are finite; a program needn't handle non-finite values.
Results may differ from a plain program's by a relative error of at most 0.0035.
Values may be sent and summed in bfloat16 or wider, within the bound.
A program may use at most 128 MiB of HBM per device.

v0:
```python
import jax
import jax.numpy as jnp
from jax import lax
from jax.sharding import PartitionSpec as P

KERNEL_WIDTH = 16
step_size = 8.0
masked_score = -1e30


def combined_all(part, axis, combine):
    gathered = jax.tree.map(lambda a: lax.all_gather(a, axis), part)

    def take(source):
        return jax.tree.map(lambda a: lax.dynamic_index_in_dim(a, source, 0, False), gathered)

    return lax.fori_loop(
        1, lax.axis_size(axis), lambda source, state: combine(state, take(source)), take(0)
    )


def square_norms(values):
    wide = values.astype(jnp.float32)
    return jnp.sum(wide * wide, axis=1)


def row_terms(row_block, row_sq, row_ids, samples, ref_sq, columns, column_sq, column_ids):
    cross_scores = (
        2.0 * jnp.einsum("rd,md->rm", row_block, samples, preferred_element_type=jnp.float32)
        - row_sq[:, None]
        - ref_sq[None, :]
    ) / (2.0 * KERNEL_WIDTH)
    cross_max = jnp.max(cross_scores, axis=1)
    cross_weights = jnp.exp(cross_scores - cross_max[:, None])
    cross_total = jnp.sum(cross_weights, axis=1)
    cross_sum = jnp.dot(
        cross_weights.astype(jnp.bfloat16), samples, preferred_element_type=jnp.float32
    )
    self_scores = (
        2.0 * jnp.einsum("rd,cd->rc", row_block, columns, preferred_element_type=jnp.float32)
        - row_sq[:, None]
        - column_sq[None, :]
    ) / (2.0 * KERNEL_WIDTH)
    diag_mask = row_ids[:, None] == column_ids[None, :]
    self_scores = jnp.where(diag_mask, masked_score, self_scores)
    self_max = jnp.max(self_scores, axis=1)
    self_weights = jnp.where(diag_mask, 0.0, jnp.exp(self_scores - self_max[:, None]))
    self_total = jnp.sum(self_weights, axis=1)
    self_sum = jnp.dot(
        self_weights.astype(jnp.bfloat16), columns, preferred_element_type=jnp.float32
    )
    return (cross_max, cross_total, cross_sum, self_max, self_total, self_sum)


def combine_parts(left_side, right_side):
    cross_top = jnp.maximum(left_side[0], right_side[0])
    left_cross = jnp.exp(left_side[0] - cross_top)
    right_cross = jnp.exp(right_side[0] - cross_top)
    self_top = jnp.maximum(left_side[3], right_side[3])
    left_self = jnp.exp(left_side[3] - self_top)
    right_self = jnp.exp(right_side[3] - self_top)
    return (
        cross_top,
        left_side[1] * left_cross + right_side[1] * right_cross,
        left_side[2] * left_cross[:, None] + right_side[2] * right_cross[:, None],
        self_top,
        left_side[4] * left_self + right_side[4] * right_self,
        left_side[5] * left_self[:, None] + right_side[5] * right_self[:, None],
    )


def per_device(particles, samples):
    part_dev = particles.shape[0]
    grp_count = lax.axis_size("grp")
    grp_pos = lax.axis_index("grp")
    ref_pos = lax.axis_index("ref")
    group = lax.all_gather(particles, "ref", axis=0, tiled=True)
    columns = lax.all_gather(particles, "grp", axis=0, tiled=True)
    group_rows = group.shape[0]
    column_ids = (
        jnp.arange(grp_count, dtype=jnp.int32)[:, None] * group_rows
        + ref_pos * part_dev
        + jnp.arange(part_dev, dtype=jnp.int32)[None, :]
    ).reshape(-1)
    row_ids = grp_pos * group_rows + jnp.arange(group_rows, dtype=jnp.int32)
    group_sq = square_norms(group)
    column_sq = square_norms(columns)
    ref_sq = square_norms(samples)
    block_rows = min(512, group_rows)
    blocks = group_rows // block_rows

    def one_block(inputs):
        row_block, row_sq, block_ids = inputs
        return row_terms(
            row_block, row_sq, block_ids, samples, ref_sq, columns, column_sq, column_ids
        )

    stacked_terms = lax.map(
        one_block,
        (
            group.reshape(blocks, block_rows, group.shape[1]),
            group_sq.reshape(blocks, block_rows),
            row_ids.reshape(blocks, block_rows),
        ),
    )
    cross_max, cross_total, cross_sum, self_max, self_total, self_sum = tuple(
        (stacked.reshape((group_rows,) + stacked.shape[2:]) for stacked in stacked_terms)
    )
    merged = combined_all(
        (cross_max, cross_total, cross_sum, self_max, self_total, self_sum), "ref", combine_parts
    )
    start = ref_pos * part_dev
    cross_mean = (
        lax.dynamic_slice_in_dim(merged[2], start, part_dev, 0)
        / lax.dynamic_slice_in_dim(merged[1], start, part_dev, 0)[:, None]
    )
    self_mean = (
        lax.dynamic_slice_in_dim(merged[5], start, part_dev, 0)
        / lax.dynamic_slice_in_dim(merged[4], start, part_dev, 0)[:, None]
    )
    return particles.astype(jnp.float32) + step_size * (cross_mean - self_mean)


def solution(mesh):
    in_specs = (P(("grp", "ref"), None), P("ref", None))
    out_specs = P(("grp", "ref"), None)
    return jax.shard_map(
        per_device, mesh=mesh, in_specs=in_specs, out_specs=out_specs, check_vma=False
    )
```

profile of v0, /device:TPU:3, one launch (start us, length us, event | category | flops | bytes accessed | tf_op | source)
XLA Modules:
  0.0 376.9 jit_solution(6727869570558348518)
XLA Ops:
  6.5 20.5 %all_gather.28 = bf16[64,512]{1,0:T(8,128)(2,1)S(1)} all-gather(bf16[8,512]{1,0:T(8,128)(2,1)} %param.4), channel_id=1, replica_groups=mesh['grp'=8,'ref'=32] {'grp'}, dimensions={0}, use_global_device_ids=true | all-gather | bytes 73728 | tf_op jit(solution)/shard_map/all_gather | solution.py:78
  27.0 54.9 %all_gather.24 = bf16[256,512]{1,0:T(8,128)(2,1)S(1)} all-gather(bf16[8,512]{1,0:T(8,128)(2,1)} %param.4), channel_id=1, replica_groups=mesh['grp'=8,'ref'=32] {'ref'}, dimensions={0}, use_global_device_ids=true | all-gather | bytes 270336 | tf_op jit(solution)/shard_map/all_gather | solution.py:77
  83.8 3.2 multiply_reduce_fusion
  88.7 2.0 copy-done.1
  90.7 2.1 fusion.7
  92.9 40.8 %all-gather.9 = f32[32,1,256]{2,1,0:T(1,128)S(1)} all-gather(f32[1,1,256]{2,1,0:T(1,128)S(1)} %bitcast.65), channel_id=6, replica_groups=mesh['grp'=8,'ref'=32] {'ref'}, dimensions={0}, use_global_device_ids=true | all-gather | bytes 33792 | tf_op jit(solution)/shard_map/all_gather | solution.py:12
  133.8 44.0 %all-gather.8 = f32[32,1,256]{2,1,0:T(1,128)S(1)} all-gather(f32[1,1,256]{2,1,0:T(1,128)S(1)} %bitcast.64), channel_id=5, replica_groups=mesh['grp'=8,'ref'=32] {'ref'}, dimensions={0}, use_global_device_ids=true | all-gather | bytes 33792 | tf_op jit(solution)/shard_map/all_gather | solution.py:12
  177.8 3.1 fusion.6
  180.9 39.5 %all-gather.7 = f32[32,1,256]{2,1,0:T(1,128)S(1)} all-gather(f32[1,1,256]{2,1,0:T(1,128)S(1)} %bitcast.67), channel_id=3, replica_groups=mesh['grp'=8,'ref'=32] {'ref'}, dimensions={0}, use_global_device_ids=true | all-gather | bytes 33792 | tf_op jit(solution)/shard_map/all_gather | solution.py:12
  220.4 40.3 %all-gather.6 = f32[32,1,256]{2,1,0:T(1,128)S(1)} all-gather(f32[1,1,256]{2,1,0:T(1,128)S(1)} %bitcast.66), channel_id=2, replica_groups=mesh['grp'=8,'ref'=32] {'ref'}, dimensions={0}, use_global_device_ids=true | all-gather | bytes 33792 | tf_op jit(solution)/shard_map/all_gather | solution.py:12
  261.8 56.3 %all-gather.13.cloned.1.call-done = f32[8192,512]{1,0:T(8,128)} async-done(((f32[256,512]{1,0:T(8,128)}), f32[8192,512]{1,0:T(8,128)}) %all-gather.13.cloned.1.call-update) | async-done | bytes 16777232 | tf_op jit(solution)/shard_map/all_gather | solution.py:12
  319.2 50.0 %while.6 = (s32[]{:T(128)}, f32[256]{0:T(256)S(1)}, f32[256]{0:T(256)S(1)}, f32[256,512]{1,0:T(8,128)S(1)}, f32[256]{0:T(256)S(1)}, /*index=5*/f32[256]{0:T(256)...) while((s32[]{:T(128)}, f32[256]{0:T(256)S(1)}, ...), condition=%wide.region_8.9_spmd, body=%wide.region_7.8_spmd.sunk | while | flops 789509 | bytes 3174603 | solution.py:17
  319.3 1.5 fusion.32
  320.9 1.5 fusion.32
  322.5 1.5 fusion.32
  325.8 1.5 fusion.32
  327.4 1.5 fusion.32
  329.0 1.5 fusion.32
  330.6 1.5 fusion.32
  333.8 1.5 fusion.32
  337.1 1.5 fusion.32
  338.7 1.5 fusion.32
  340.3 1.5 fusion.32
  341.9 1.5 fusion.32
  345.1 1.5 fusion.32
  348.4 1.5 fusion.32
  351.6 1.5 fusion.32
  353.2 1.5 fusion.32
  354.8 1.5 fusion.32
  356.4 1.5 fusion.32
  359.7 1.5 fusion.32
  362.9 1.5 fusion.32
  (230 shorter events, 25.5 us)
Async XLA Ops:
  6.5 254.2 %all-gather.15.cloned.1.call-start = ((), (), s32[]{:S(2)}) async-start(), calls=%async_computation.1 | async-start | bytes 17301504 | tf_op jit(solution)/shard_map/all_gather | solution.py:12
  83.7 234.4 %all-gather.13.cloned.1.call-start = ((), (), s32[]{:S(2)}) async-start(), calls=%async_computation | async-start | bytes 17301504 | tf_op jit(solution)/shard_map/all_gather | solution.py:12
  83.7 3.5 copy-start
  88.6 2.1 copy-start.1
  319.2 50.2 %copy-start.2 = (bf16[8,512]{1,0:T(8,128)(2,1)S(1)}, bf16[8,512]{1,0:T(8,128)(2,1)}, u32[]{:S(2)}) copy-start(bf16[8,512]{1,0:T(8,128)(2,1)} %param.4) | copy-start | bytes 24580
Sparse Core Ops, SparseCore 0:
  83.8 114.7 all-gather.14
  201.2 116.8 all-gather.12
where the time goes:
time: 378 us; the launch traced here: 377 us
  blocking collectives  240 us (63%)
  waiting for transfers between devices  56.3 us (15%)
  other arithmetic  54.2 us (14%)
  between operations  13.5 us (4%)
  local copies, waits for them, and re-layouts  6.1 us (2%)
  matrix products  4.92 us (1%)
    all_gather x4, blocking collectives, combined_all(): gathered = jax.tree.map(lambda a: lax.all_gather(a, axis), part)  165 us
    all_gather x2, waiting for transfers between devices, combined_all(): gathered = jax.tree.map(lambda a: lax.all_gather(a, axis), part)  56.3 us
    all_gather x1, blocking collectives, per_device(): group = lax.all_gather(particles, 'ref', axis=0, tiled=True)  54.9 us
    add x31, other arithmetic, combine_parts(): left_side[5] * left_self[:, None] + right_side[5] * right_self[:, None]  45.5 us
    all_gather x1, blocking collectives, per_device(): columns = lax.all_gather(particles, 'grp', axis=0, tiled=True)  20.5 us
  transfers between devices with their start and end apart: 2, of which 1 were waited for; matrix products, arithmetic and copies ran while one was open for 3% of the time, Pallas kernels for 0%

commit v1 on v0

--- a/solution.py
+++ b/solution.py
@@ -1,3 +1,4 @@
+import functools
 import jax
 import jax.numpy as jnp
 from jax import lax
@@ -6,6 +7,17 @@
 KERNEL_WIDTH = 16
 step_size = 8.0
 masked_score = -1e30
+
+
+def mix_array(chunk, shard_axis, dim_i):
+    carry_out = lax.axis_size(shard_axis)
+    block_out = jnp.stack([chunk] * carry_out, axis=0)
+    base_arr = lax.all_to_all(block_out, shard_axis, 0, 0)
+    r1 = jnp.concatenate(base_arr, axis=dim_i)
+    return r1
+
+
+chains_answer = functools.partial(mix_array, shard_axis="ref", dim_i=0)
 
 
 def combined_all(part, axis, combine):
@@ -74,7 +86,7 @@
     grp_count = lax.axis_size("grp")
     grp_pos = lax.axis_index("grp")
     ref_pos = lax.axis_index("ref")
-    group = lax.all_gather(particles, "ref", axis=0, tiled=True)
+    group = chains_answer(particles)
     columns = lax.all_gather(particles, "grp", axis=0, tiled=True)
     group_rows = group.shape[0]
     column_ids = (

time: 378 us -> 350 us (0.926); the launches traced: 377 us -> 344 us
  blocking collectives: 240 us -> 200 us
  starting transfers between devices: 0.04 us -> 12 us
  waiting for transfers between devices: 56.3 us -> 50.1 us
    all_gather x1 -> x0, blocking collectives: 54.9 us -> none  [per_device(): group = lax.all_gather(particles, 'ref', axis=0, tiled=True)]
    all_gather x4, blocking collectives: 165 us -> 177 us  [combined_all(): gathered = jax.tree.map(lambda a: lax.all_gather(a, axis), part)]
    all_to_all x0 -> x1, starting transfers between devices: none -> 11.9 us  [mix_array(): base_arr = lax.all_to_all(block_out, shard_axis, 0, 0)]
    all_gather x2, waiting for transfers between devices: 56.3 us -> 50.1 us  [combined_all(): gathered = jax.tree.map(lambda a: lax.all_gather(a, axis), part)]
  transfers between devices with their start and end apart: 2 -> 3, of which waited for: 1 -> 1; matrix products, arithmetic and copies ran while one was open for 3% -> 3% of each run, Pallas kernels for 0% -> 0%
where the time goes in v1:
time: 350 us; the launch traced here: 344 us
  blocking collectives  200 us (57%)
  other arithmetic  54.2 us (15%)
  waiting for transfers between devices  50.1 us (14%)
  between operations  13.5 us (4%)
  starting transfers between devices  12 us (3%)
  local copies, waits for them, and re-layouts  7.61 us (2%)
  matrix products  4.91 us (1%)
    all_gather x4, blocking collectives, combined_all(): gathered = jax.tree.map(lambda a: lax.all_gather(a, axis), part)  177 us
    all_gather x2, waiting for transfers between devices, combined_all(): gathered = jax.tree.map(lambda a: lax.all_gather(a, axis), part)  50.1 us
    add x31, other arithmetic, combine_parts(): left_side[5] * left_self[:, None] + right_side[5] * right_self[:, None]  45.5 us
    all_gather x1, blocking collectives, per_device(): columns = lax.all_gather(particles, 'grp', axis=0, tiled=True)  22.9 us
    all_to_all x1, starting transfers between devices, mix_array(): base_arr = lax.all_to_all(block_out, shard_axis, 0, 0)  11.9 us
  transfers between devices with their start and end apart: 3, of which 1 were waited for; matrix products, arithmetic and copies ran while one was open for 3% of the time, Pallas kernels for 0%

profile of v1, /device:TPU:3, one launch (start us, length us, event | category | flops | bytes accessed | tf_op | source)
XLA Modules:
  0.0 344.5 jit_solution(7723811195916477412)
XLA Ops:
  7.9 11.9 %all-to-all-start = ((bf16[32,8,512]{2,1,0:T(8,128)(2,1)}), bf16[32,8,512]{2,1,0:T(8,128)(2,1)S(1)}, u32[]{:S(2)}, u32[]{:S(2)}) async-start(bf16[32,8,512]{2,1,0:T(8,128)(2,1)} %stack.2), calls=%async_computation | async-start | bytes 524288 | tf_op jit(solution)/shard_map/all_to_all | solution.py:15
  20.1 22.9 %all_gather.24 = bf16[64,512]{1,0:T(8,128)(2,1)S(1)} all-gather(bf16[8,512]{1,0:T(8,128)(2,1)} %param.4), channel_id=1, replica_groups=mesh['grp'=8,'ref'=32] {'grp'}, dimensions={0}, use_global_device_ids=true | all-gather | bytes 73728 | tf_op jit(solution)/shard_map/all_gather | solution.py:90
  44.8 3.2 multiply_reduce_fusion
  49.6 2.0 copy-done.1
  51.7 2.1 fusion.7
  53.9 52.3 %all-gather.9 = f32[32,1,256]{2,1,0:T(1,128)S(1)} all-gather(f32[1,1,256]{2,1,0:T(1,128)S(1)} %bitcast.72), channel_id=6, replica_groups=mesh['grp'=8,'ref'=32] {'ref'}, dimensions={0}, use_global_device_ids=true | all-gather | bytes 33792 | tf_op jit(solution)/shard_map/all_gather | solution.py:24
  106.2 42.0 %all-gather.8 = f32[32,1,256]{2,1,0:T(1,128)S(1)} all-gather(f32[1,1,256]{2,1,0:T(1,128)S(1)} %bitcast.71), channel_id=5, replica_groups=mesh['grp'=8,'ref'=32] {'ref'}, dimensions={0}, use_global_device_ids=true | all-gather | bytes 33792 | tf_op jit(solution)/shard_map/all_gather | solution.py:24
  148.2 3.1 fusion.6
  151.3 42.7 %all-gather.7 = f32[32,1,256]{2,1,0:T(1,128)S(1)} all-gather(f32[1,1,256]{2,1,0:T(1,128)S(1)} %bitcast.74), channel_id=3, replica_groups=mesh['grp'=8,'ref'=32] {'ref'}, dimensions={0}, use_global_device_ids=true | all-gather | bytes 33792 | tf_op jit(solution)/shard_map/all_gather | solution.py:24
  194.0 40.5 %all-gather.6 = f32[32,1,256]{2,1,0:T(1,128)S(1)} all-gather(f32[1,1,256]{2,1,0:T(1,128)S(1)} %bitcast.73), channel_id=2, replica_groups=mesh['grp'=8,'ref'=32] {'ref'}, dimensions={0}, use_global_device_ids=true | all-gather | bytes 33792 | tf_op jit(solution)/shard_map/all_gather | solution.py:24
  235.6 50.1 %all-gather.13.cloned.1.call-done = f32[8192,512]{1,0:T(8,128)} async-done(((f32[256,512]{1,0:T(8,128)}), f32[8192,512]{1,0:T(8,128)}) %all-gather.13.cloned.1.call-update) | async-done | bytes 16777232 | tf_op jit(solution)/shard_map/all_gather | solution.py:24
  286.8 50.0 %while.6 = (s32[]{:T(128)}, f32[256]{0:T(256)S(1)}, f32[256]{0:T(256)S(1)}, f32[256,512]{1,0:T(8,128)S(1)}, f32[256]{0:T(256)S(1)}, /*index=5*/f32[256]{0:T(256)...) while((s32[]{:T(128)}, f32[256]{0:T(256)S(1)}, ...), condition=%wide.region_8.9_spmd, body=%wide.region_7.8_spmd.sunk | while | flops 789509 | bytes 3174603 | solution.py:29
  286.9 1.5 fusion.32
  288.5 1.5 fusion.32
  291.7 1.5 fusion.32
  295.0 1.5 fusion.32
  296.6 1.5 fusion.32
  298.2 1.5 fusion.32
  299.8 1.5 fusion.32
  303.0 1.5 fusion.32
  304.6 1.5 fusion.32
  306.3 1.5 fusion.32
  307.9 1.5 fusion.32
  311.1 1.5 fusion.32
  312.7 1.5 fusion.32
  314.3 1.5 fusion.32
  317.6 1.5 fusion.32
  319.2 1.5 fusion.32
  320.8 1.5 fusion.32
  322.4 1.5 fusion.32
  325.6 1.5 fusion.32
  328.9 1.5 fusion.32
  (233 shorter events, 27.0 us)
Async XLA Ops:
  7.9 35.1 %all-to-all-start = ((bf16[32,8,512]{2,1,0:T(8,128)(2,1)}), bf16[32,8,512]{2,1,0:T(8,128)(2,1)S(1)}, u32[]{:S(2)}, u32[]{:S(2)}) async-start(bf16[32,8,512]{2,1,0:T(8,128)(2,1)} %stack.2), calls=%async_computation | async-start | bytes 524288 | tf_op jit(solution)/shard_map/all_to_all | solution.py:15
  19.9 214.6 %all-gather.15.cloned.1.call-start = ((), (), s32[]{:S(2)}) async-start(), calls=%async_computation.2 | async-start | bytes 17301504 | tf_op jit(solution)/shard_map/all_gather | solution.py:24
  44.7 241.0 %all-gather.13.cloned.1.call-start = ((), (), s32[]{:S(2)}) async-start(), calls=%async_computation.1 | async-start | bytes 17301504 | tf_op jit(solution)/shard_map/all_gather | solution.py:24
  44.7 3.5 %copy-start = (bf16[4096,512]{1,0:T(8,128)(2,1)S(1)}, bf16[4096,512]{1,0:T(8,128)(2,1)}, u32[]{:S(2)}) copy-start(bf16[4096,512]{1,0:T(8,128)(2,1)} %param.5) | copy-start | bytes 12582916
  49.6 2.1 copy-start.1
  286.8 50.2 %copy-start.2 = (bf16[8,512]{1,0:T(8,128)(2,1)S(1)}, bf16[8,512]{1,0:T(8,128)(2,1)}, u32[]{:S(2)}) copy-start(bf16[8,512]{1,0:T(8,128)(2,1)} %param.4) | copy-start | bytes 24580
Sparse Core Ops, SparseCore 0:
  44.8 117.5 all-gather.14
  165.0 120.6 all-gather.12
